TPU v7x, 128 devices: a whole 4x4x4 slice. The times are simulated.
128 devices in a mesh: req: 8 (over x, y_hi), hid: 16 (over y_lo, z, core).
Axes of the slice: x: 4, y: 4 (y_hi: 2, y_lo: 2; y = y_hi * 2 + y_lo), z: 4, core: 2. Of those that a mesh axis runs over, the one named last changes fastest.
Arguments:
- input_activations: bfloat16 [8, 512, 4096], P('req'), may hold values from -6 to 6
- prompt_extents: int32 [8], P('req'), may hold values from 1 to 512, as said below
- continuing_flags: int32 [8], P('req'), may hold values from 0 to 1, as said below
- owning_index: int32 [8], P('req'), may hold values from 0 to 15
- partition_arrangement: int32 [128], replicated, may hold values from 0 to 127, each once
- training_accept_pieces: float32 [4096, 4096], P(('req', 'hid')), may hold values from -0.09375 to 0.09375
- training_lookup_pieces: float32 [4096, 4096], P(('req', 'hid')), may hold values from -0.09375 to 0.09375
- training_content_pieces: float32 [4096, 4096], P(('req', 'hid')), may hold values from -0.09375 to 0.09375
- normalizer_scales: bfloat16 [2, 4096], replicated, may hold values from 0.5 to 1.5
- prior_step_blends: bfloat16 [7, 4096], replicated, may hold values from 0.049804688 to 0.94921875
- forgetting_bias_vector: float32 [4096], P('hid'), may hold values from -7 to -3
- forgetting_left_lowrank: bfloat16 [4096, 128], replicated, may hold values from -0.09375 to 0.09375
- forgetting_right_lowrank: bfloat16 [128, 4096], P(None, 'hid'), may hold values from -0.5 to 0.5
- instant_emphasis: float32 [4096], P('hid'), may hold values from -3 to 3
- group_normalizer_scale: float32 [4096], P('hid'), may hold values from 0.5 to 1.5
- gating_projection: bfloat16 [4096, 4096], P(None, 'hid'), may hold values from -0.09375 to 0.09375
- mixing_exit_projection: bfloat16 [4096, 4096], P('hid'), may hold values from -0.09375 to 0.09375
- kept_summary_places: float32 [8, 16, 64, 64, 64], P('req', 'hid'), may hold values from -6 to 6
- previous_normed_entries: bfloat16 [8, 2, 4096], P('req'), may hold values from -6 to 6
- feedforward_entry_proj: bfloat16 [14336, 4096], P(('req', 'hid')), may hold values from -0.09375 to 0.09375
- feedforward_exit_proj: bfloat16 [14336, 4096], P(('req', 'hid')), may hold values from -0.046875 to 0.046875
- feedforward_accept_proj: bfloat16 [4096, 4096], P(None, 'hid'), may hold values from -0.09375 to 0.09375
Outputs:
- layer_out: bfloat16 [8, 512, 4096], P('req', None, 'hid')
- new_states: float32 [8, 64, 64, 64], P('req', 'hid')
- new_shift: bfloat16 [8, 2, 4096], P('req')
Inputs may be any that keep to these rules, and one draw needn't show every extreme that they name: `prompt_extents`: in every draw some request has length 512. `continuing_flags`: at least one request has 1 and at least one has 0. `owning_index`: read only where continuing_flags is 1. `partition_arrangement`: each of 0 to 127 appears once.
All inputs are finite; a program needn't handle non-finite values.
Results may differ from a plain program's by a relative error of at most 0.02.
Values may be sent and summed in bfloat16 or wider, within the bound.
A program may use at most 192 MiB of HBM per device.

v0:
```python
from functools import partial
import jax
import jax.numpy as jnp
from jax import lax
from jax.sharding import PartitionSpec as P

GROUP_DIMENSION = 64


def layer_norm(values, gain):
    center = values - jnp.mean(values, axis=-1, keepdims=True)
    spread = jnp.mean(center * center, axis=-1, keepdims=True)
    return center / jnp.sqrt(spread + 1e-05) * gain


def head_norm(outputs, gain_rows):
    center = outputs - jnp.mean(outputs, axis=-1, keepdims=True)
    spread = jnp.mean(center * center, axis=-1, keepdims=True)
    return center / jnp.sqrt(spread + 0.00064) * gain_rows


def shifted(values, first_row):
    return jnp.concatenate([first_row[None, :], values[:-1]], axis=0)


def segment_step(extra_diagonal_term, carried_summary, piece_sequence):
    acceptance_vectors, present_lookup_vectors, content_vectors, decays = piece_sequence
    inclusive = jnp.cumsum(decays, axis=0)
    exclusive = inclusive - decays
    closing = inclusive[-1]
    resulting_activations = jnp.einsum(
        "thi,hij->thj",
        acceptance_vectors * jnp.exp(exclusive),
        carried_summary,
        precision=lax.Precision.HIGHEST,
    )
    distance = exclusive[:, None] - inclusive[None, :]
    sizing = decays.shape[0]
    earlier = (jnp.arange(sizing)[:, None] > jnp.arange(sizing)[None, :]).astype(jnp.float32)
    factor = jnp.exp(jnp.minimum(distance, 0.0)) * earlier[:, :, None, None]
    scores = jnp.sum(
        acceptance_vectors[:, None] * factor * present_lookup_vectors[None, :], axis=-1
    )
    resulting_activations = resulting_activations + jnp.einsum(
        "tsh,shj->thj", scores, content_vectors, precision=lax.Precision.HIGHEST
    )
    resulting_activations = (
        resulting_activations
        + jnp.sum(
            acceptance_vectors * extra_diagonal_term * present_lookup_vectors,
            axis=-1,
            keepdims=True,
        )
        * content_vectors
    )
    weighted = present_lookup_vectors * jnp.exp(closing[None] - inclusive)
    carried_summary = jnp.exp(closing)[:, :, None] * carried_summary + jnp.einsum(
        "shi,shj->hij", weighted, content_vectors, precision=lax.Precision.HIGHEST
    )
    return (carried_summary, resulting_activations)


def local(
    input_activations,
    prompt_extents,
    continuing_flags,
    owning_index,
    partition_arrangement,
    training_accept_pieces,
    training_lookup_pieces,
    training_content_pieces,
    normalizer_scales,
    prior_step_blends,
    forgetting_bias_vector,
    forgetting_left_lowrank,
    forgetting_right_lowrank,
    instant_emphasis,
    group_normalizer_scale,
    gating_projection,
    mixing_exit_projection,
    kept_summary_places,
    previous_normed_entries,
    feedforward_entry_proj,
    feedforward_exit_proj,
    feedforward_accept_proj,
):
    token_rows = input_activations[0]
    seq_len, width = token_rows.shape
    local_width = mixing_exit_projection.shape[0]
    groups_on_device = local_width // GROUP_DIMENSION
    shards = partition_arrangement.shape[0]
    shard_rows = width // shards
    length = prompt_extents[0]
    resuming = continuing_flags[0]
    present = jnp.arange(seq_len) < length
    gain_rows = normalizer_scales.astype(jnp.float32)
    mix_rows = prior_step_blends.astype(jnp.float32)
    carried = previous_normed_entries[0].astype(jnp.float32)
    normed_in = layer_norm(token_rows.astype(jnp.float32), gain_rows[0])
    before = shifted(normed_in, jnp.where(resuming == 1, carried[0], 0.0))
    blended = (normed_in[None] + (before - normed_in)[None] * mix_rows[:5, None, :]).astype(
        jnp.bfloat16
    )
    permuted = jnp.take(
        blended[:3].reshape(3, seq_len, shards, shard_rows), partition_arrangement, axis=2
    ).reshape(3, seq_len, width)
    local_rows = jnp.stack(
        [training_accept_pieces, training_lookup_pieces, training_content_pieces]
    ).astype(jnp.bfloat16)
    collected = lax.all_gather(local_rows, "req", axis=1, tiled=True)
    swapped = lax.all_to_all(collected, "hid", split_axis=2, concat_axis=1, tiled=True)
    hid_count = lax.axis_size("hid")
    req_count = lax.axis_size("req")
    ordered = (
        swapped.reshape(3, hid_count, req_count, shard_rows, local_width)
        .transpose(0, 2, 1, 3, 4)
        .reshape(3, width, local_width)
    )
    projected = jnp.einsum("mtd,mdc->mtc", permuted, ordered, preferred_element_type=jnp.float32)
    low_rank = jnp.tanh(
        jnp.dot(blended[3], forgetting_left_lowrank, preferred_element_type=jnp.float32)
    ).astype(jnp.bfloat16)
    log_decay = -jnp.exp(
        forgetting_bias_vector
        + jnp.dot(low_rank, forgetting_right_lowrank, preferred_element_type=jnp.float32)
    )
    log_decay = jnp.where(present[:, None], log_decay, 0.0)
    gate = jax.nn.silu(jnp.dot(blended[4], gating_projection, preferred_element_type=jnp.float32))
    present_lookup_vectors = jnp.where(present[:, None], projected[1], 0.0)
    fetched = lax.all_to_all(
        kept_summary_places.astype(jnp.bfloat16), "hid", split_axis=2, concat_axis=1, tiled=True
    ).astype(kept_summary_places.dtype)
    chosen = lax.dynamic_index_in_dim(fetched[0], owning_index[0], 0, keepdims=False)
    carried_summary = jnp.where(resuming == 1, chosen, 0.0)
    block_len = min(64, seq_len)
    count_blocks = seq_len // block_len

    def by_blocks(values):
        return values.reshape(count_blocks, block_len, groups_on_device, GROUP_DIMENSION)

    sequences = (
        by_blocks(projected[0]),
        by_blocks(present_lookup_vectors),
        by_blocks(projected[2]),
        by_blocks(log_decay),
    )
    segment_cursor = partial(
        segment_step, instant_emphasis.reshape(groups_on_device, GROUP_DIMENSION)
    )
    carried_summary, outputs = lax.scan(segment_cursor, carried_summary, sequences)
    outputs = outputs.reshape(seq_len, groups_on_device, GROUP_DIMENSION)
    grouped = head_norm(
        outputs, group_normalizer_scale.reshape(groups_on_device, GROUP_DIMENSION)
    ).reshape(seq_len, local_width)
    gated = (grouped * gate).astype(jnp.bfloat16)
    head_terms = jnp.dot(gated, mixing_exit_projection, preferred_element_type=jnp.float32)
    attended = lax.psum(head_terms.astype(jnp.bfloat16), "hid").astype(jnp.float32)
    middle = (token_rows.astype(jnp.float32) + attended).astype(jnp.bfloat16)
    mid_share = lax.dynamic_slice_in_dim(
        middle, lax.axis_index("hid") * local_width, local_width, 1
    )
    chan_in = layer_norm(middle.astype(jnp.float32), gain_rows[1])
    chan_before = shifted(chan_in, jnp.where(resuming == 1, carried[1], 0.0))
    chan_mixed = (chan_in[None] + (chan_before - chan_in)[None] * mix_rows[5:, None, :]).astype(
        jnp.bfloat16
    )
    key_rows = lax.all_gather(feedforward_entry_proj, "req", axis=0, tiled=True)
    value_rows = lax.all_gather(feedforward_exit_proj, "req", axis=0, tiled=True)
    inner = lax.dot_general(
        chan_mixed[0], key_rows, (((1,), (1,)), ((), ())), preferred_element_type=jnp.float32
    )
    hidden = jnp.square(jnp.maximum(inner, 0.0)).astype(jnp.bfloat16)
    channel_terms = jnp.dot(hidden, value_rows, preferred_element_type=jnp.float32)
    mixed_out = lax.psum_scatter(
        channel_terms.astype(jnp.bfloat16), "hid", scatter_dimension=1, tiled=True
    ).astype(jnp.float32)
    gate_rows = jax.nn.sigmoid(
        jnp.dot(chan_mixed[1], feedforward_accept_proj, preferred_element_type=jnp.float32)
    )
    combined = mid_share.astype(jnp.float32) + gate_rows * mixed_out
    layer_out = jnp.where(present[:, None], combined, 0.0).astype(jnp.bfloat16)[None]
    last_index = length - 1
    shift_out = jnp.stack(
        [
            lax.dynamic_index_in_dim(normed_in, last_index, 0, keepdims=False),
            lax.dynamic_index_in_dim(chan_in, last_index, 0, keepdims=False),
        ]
    ).astype(jnp.bfloat16)[None]
    return (layer_out, carried_summary[None], shift_out)


def solution(mesh):
    placed = (
        P("req", None, None),
        P("req"),
        P("req"),
        P("req"),
        P(),
        P(("req", "hid"), None),
        P(("req", "hid"), None),
        P(("req", "hid"), None),
        P(),
        P(),
        P("hid"),
        P(),
        P(None, "hid"),
        P("hid"),
        P("hid"),
        P(None, "hid"),
        P("hid", None),
        P("req", "hid", None, None, None),
        P("req", None, None),
        P(("req", "hid"), None),
        P(("req", "hid"), None),
        P(None, "hid"),
    )
    return jax.shard_map(
        local,
        mesh=mesh,
        in_specs=placed,
        out_specs=(P("req", None, "hid"), P("req", "hid", None, None), P("req", None, None)),
        check_vma=False,
    )
```

profile of v0, /device:TPU:6, one launch (start us, length us, event | category | flops | bytes accessed | tf_op | source)
XLA Modules:
  0.0 817.3 jit_solution(10165721648546910749)
XLA Ops:
  7.2 1.2 convert_bitcast_fusion.3
  8.4 1.3 convert_bitcast_fusion.1
  10.7 1.8 fusion.60
  12.5 1.5 reshape.260
  14.0 6.4 all-to-all-start
  21.3 3.4 convert_reduce_fusion
  24.8 3.4 fusion.19
  28.3 1.8 fusion.20
  30.1 4.1 slice_bitcast_fusion.1
  34.2 1.7 copy-done.5
  36.6 67.1 %all-gather.4.cloned.1.call-done = bf16[3,256,4096]{2,1,0:T(8,128)(2,1)} async-done(((bf16[3,32,4096]{2,1,0:T(8,128)(2,1)}), bf16[3,256,4096]{2,1,0:T(8,128)(2,1)}) %all-gather.4.cloned.1.call-update) | async-done | bytes 6291472 | tf_op jit(solution)/shard_map/all_gather | solution.py:110
  103.7 13.1 %copy.123 = bf16[3,256,4096]{1,0,2:T(4,128)(2,1)} copy(bf16[3,256,4096]{2,1,0:T(8,128)(2,1)} %all-gather.4.cloned.1.call-done) | data formatting | bytes 12582912 | tf_op jit(solution)/shard_map/all_gather | solution.py:110
  116.8 4.8 all-to-all-start.1
  121.9 10.4 %fusion.27 = (f32[512,4096]{1,0:T(8,128)}, f32[512,4096]{1,0:T(8,128)}) fusion(bf16[1,512,4096]{2,1,0:T(8,128)(2,1)} %param.24, f32[4096]{0:T(1024)S(1)} %bitcast.201, f32[512]{0:T(512)S(1)} %add_sqrt_fusion.1, f32[512]{0:T(512)S(1)} %broadcast_multiply_fusion.1, f32[1,511,4096]{2,1,0:T(8,128)} %slice_bitcast_fusion.1, f32[1,1,4096]{2,1,0:T(1,128)S(1)} %get-tuple-element.126), kind=kLoop, calls=%fused_computation.55 | loop fusion | flops 12582912 | bytes 29380608 | tf_op jit(solution)/shard_map/add | solution.py:101
  132.3 9.0 %copy.120 = f32[512,4096]{0,1:T(8,128)} copy(f32[512,4096]{1,0:T(8,128)} %get-tuple-element.120) | data formatting | bytes 16777216 | tf_op jit(solution)/shard_map/add | solution.py:101
  141.3 9.0 %copy.121 = f32[512,4096]{0,1:T(8,128)} copy(f32[512,4096]{1,0:T(8,128)} %get-tuple-element.121) | data formatting | bytes 16777216 | tf_op jit(solution)/shard_map/mul | solution.py:101
  150.4 10.3 %add_convert_fusion = bf16[5,512,4096]{1,2,0:T(8,128)(2,1)S(1)} fusion(f32[5,4096]{1,0:T(8,128)S(1)} %slice.75, f32[512,4096]{0,1:T(8,128)} %copy.121, f32[512,4096]{0,1:T(8,128)} %copy.120), kind=kLoop, calls=%fused_computation.28 | loop fusion | flops 31457280 | bytes 37830656 | tf_op jit(solution)/shard_map/convert_element_type | solution.py:101
  160.7 6.5 slice.77
  167.2 4.2 copy-done.4
  171.4 12.8 %gather_fusion = bf16[128,3,512,32]{2,3,1,0:T(8,128)(2,1)} fusion(bf16[3,512,128,32]{1,3,2,0:T(8,128)(2,1)} %bitcast.190, s32[1024]{0:T(1024)S(1)} %pad_clamp_fusion), kind=kCustom, calls=%fused_computation | custom fusion | bytes 25166336 | tf_op jit(solution)/shard_map/jit(_take)/gather | solution.py:104
  184.2 10.7 %copy.122 = bf16[3,512,128,32]{1,3,2,0:T(8,128)(2,1)} copy(bf16[3,512,128,32]{1,3,0,2:T(8,128)(2,1)} %bitcast.191) | data formatting | bytes 25165824 | tf_op jit(solution)/shard_map/jit(_take)/gather | solution.py:104
  195.8 3.9 fusion.34
  199.8 1.5 reshape.245
  202.5 11.2 %bitcast_select_fusion = bf16[3,512,4096]{1,2,0:T(8,128)(2,1)} fusion(bf16[3,512,128,32]{1,3,2,0:T(8,128)(2,1)} %copy.122, pred[4096]{0:T(1024)(128)(4,1)S(1)} %broadcast_in_dim.95), kind=kLoop, calls=%fused_computation.30 | loop fusion | flops 6291456 | bytes 25169920 | tf_op jit(solution)/shard_map/jit(_take)/select_n | solution.py:104
  213.7 1.7 reshape.261
  216.2 27.1 %all-to-all-done.1 = bf16[3,256,4096]{1,0,2:T(4,128)(2,1)} async-done(((bf16[3,256,4096]{1,0,2:T(4,128)(2,1)}), bf16[3,256,4096]{1,0,2:T(4,128)(2,1)}, u32[]{:S(2)}, u32[]{:S(2)}) %all-to-all-start.1) | async-done | bytes 6291488 | tf_op jit(solution)/shard_map/all_to_all | solution.py:111
  243.3 6.9 copy.124
  250.2 9.1 %copy.125 = bf16[3,16,256,256]{3,2,1,0:T(8,128)(2,1)} copy(bf16[3,16,256,256]{2,3,1,0:T(8,128)(2,1)} %bitcast.193) | data formatting | bytes 12582912 | tf_op jit(solution)/shard_map/all_to_all | solution.py:111
  259.3 6.5 copy.126
  265.7 12.0 %fusion.61 = f32[3,512,256]{2,1,0:T(8,128)} fusion(bf16[3,512,4096]{1,2,0:T(8,128)(2,1)} %bitcast_select_fusion, bf16[3,4096,256]{2,1,0:T(8,128)(2,1)} %bitcast.196), kind=kOutput, calls=%fused_computation.119 | convolution fusion | flops 3221225472 | bytes 20447232 | tf_op jit(solution)/shard_map/mtd,mdc->mtc/dot_general | solution.py:119
  277.7 2.6 fusion.58
  280.2 1.5 squeeze.51
  281.7 2.5 reshape_squeeze.6
  284.2 2.4 reshape_squeeze.7
  286.6 1.5 broadcast_select_fusion
  288.1 79.8 %while.12 = (s32[]{:T(128)}, f32[4,64,64]{2,1,0:T(8,128)S(1)}, f32[8,64,4,64]{3,1,2,0:T(8,128)}, f32[8,64,4,64]{3,2,1,0:T(4,128)}, f32[8,64,4,64]{3,2,1,0:T(4,12...) while((s32[]{:T(128)}, f32[4,64,64]{2,1,0:T(8,128)S(1)}, ...), condition=%wide.region_6.7_spmd, body=%wide.region_2.6_spmd.sunk | while | flops 45260544 | bytes 2537577 | solution.py:150
  292.0 3.4 multiply_reduce_fusion.6
  302.0 3.4 multiply_reduce_fusion.6
  308.8 1.1 multiply_reduce_fusion.5
  311.9 3.4 multiply_reduce_fusion.6
  318.7 1.1 multiply_reduce_fusion.5
  321.9 3.4 multiply_reduce_fusion.6
  328.6 1.1 multiply_reduce_fusion.5
  331.8 3.4 multiply_reduce_fusion.6
  338.6 1.1 multiply_reduce_fusion.5
  341.8 3.4 multiply_reduce_fusion.6
  351.7 3.4 multiply_reduce_fusion.6
  361.7 3.4 multiply_reduce_fusion.6
  367.9 2.0 copy.130
  369.8 1.6 reduce_sum.74
  371.5 1.4 reshape.249
  372.9 1.9 multiply_reduce_fusion.2
  376.3 9.6 %convolution_convert_fusion.1 = bf16[512,4096]{1,0:T(8,128)(2,1)} fusion(bf16[256,4096]{1,0:T(8,128)(2,1)S(1)} %copy-done, bf16[4096,256]{1,0:T(8,128)(2,1)} %param.39, bf16[5,512,4096]{1,2,0:T(8,128)(2,1)} %copy-done.4, f32[512,256]{1,0:T(8,128)S(1)} %copy.135, f32[512,256]{1,0:T(8,128)} %reshape.249, f32[512,256]{1,0:T(8,128)} %copy.132, ...), kind=kOutput, calls=%fused_computation.54 | convolution fusion | flops 2150760448 | bytes 14156800 | tf_op jit(solution)/shard_map/dot_general | solution.py:156
  387.2 135.4 %all-reduce.2.cloned.1.call-done = bf16[512,4096]{1,0:T(8,128)(2,1)} async-done(((bf16[512,4096]{1,0:T(8,128)(2,1)}), bf16[512,4096]{1,0:T(8,128)(2,1)}) %all-reduce.2.cloned.1.call-update) | async-done | bytes 4194320 | tf_op jit(solution)/shard_map/psum | solution.py:157
  522.7 5.2 convert_reduce_fusion.1
  527.9 1.2 fusion.21
  529.1 2.1 fusion.22
  531.2 3.5 maximum_subtract_fusion.1
  534.7 4.8 add_convert_fusion.1
  539.5 83.5 %all-gather.6.cloned.1.call-done = bf16[896,4096]{1,0:T(8,128)(2,1)} async-done(((bf16[112,4096]{1,0:T(8,128)(2,1)}), bf16[896,4096]{1,0:T(8,128)(2,1)}) %all-gather.6.cloned.1.call-update) | async-done | bytes 7340048 | tf_op jit(solution)/shard_map/all_gather | solution.py:167
  623.0 99.4 %all-gather.8.cloned.1.call-done = bf16[896,4096]{1,0:T(8,128)(2,1)} async-done(((bf16[112,4096]{1,0:T(8,128)(2,1)}), bf16[896,4096]{1,0:T(8,128)(2,1)}) %all-gather.8.cloned.1.call-update) | async-done | bytes 7340048 | tf_op jit(solution)/shard_map/all_gather | solution.py:168
  722.4 16.2 %convolution_convert_fusion = bf16[512,4096]{1,0:T(8,128)(2,1)} fusion(bf16[896,4096]{1,0:T(8,128)(2,1)} %all-gather.8.cloned.1.call-done, bf16[896,4096]{1,0:T(8,128)(2,1)} %all-gather.6.cloned.1.call-done, bf16[2,512,4096]{2,1,0:T(8,128)(2,1)} %add_convert_fusion.1), kind=kOutput, calls=%fused_computation.53 | convolution fusion | flops 7519666176 | bytes 23068672 | tf_op jit(solution)/shard_map/dot_general | solution.py:173
  741.1 64.5 %reduce-scatter.2.cloned.1.call-done = bf16[512,256]{1,0:T(8,128)(2,1)} async-done(((bf16[512,4096]{1,0:T(8,128)(2,1)}), bf16[512,256]{1,0:T(8,128)(2,1)}) %reduce-scatter.2.cloned.1.call-update) | async-done | bytes 262160 | tf_op jit(solution)/shard_map/reduce_scatter | solution.py:174
  805.6 4.9 fusion.45
  (186 shorter events, 56.6 us)
Async XLA Ops:
  7.2 369.1 %copy-start = (bf16[256,4096]{1,0:T(8,128)(2,1)S(1)}, bf16[256,4096]{1,0:T(8,128)(2,1)}, u32[]{:S(2)}) copy-start(bf16[256,4096]{1,0:T(8,128)(2,1)} %param.40) | copy-start | bytes 6291460
  7.2 14.1 %copy-start.11 = (bf16[1,2,4096]{2,1,0:T(2,128)(2,1)S(1)}, bf16[1,2,4096]{2,1,0:T(2,128)(2,1)}, u32[]{:S(2)}) copy-start(bf16[1,2,4096]{2,1,0:T(2,128)(2,1)} %param.42) | copy-start | bytes 49156
  7.2 96.5 %all-gather.4.cloned.1.call-start = ((), (), s32[]{:S(2)}) async-start(), calls=%async_computation.3 | async-start | bytes 7077888 | tf_op jit(solution)/shard_map/all_gather | solution.py:110
  9.7 18.5 %copy-start.9 = (bf16[2,4096]{1,0:T(2,128)(2,1)S(1)}, bf16[2,4096]{1,0:T(2,128)(2,1)}, u32[]{:S(2)}) copy-start(bf16[2,4096]{1,0:T(2,128)(2,1)} %param.32) | copy-start | bytes 49156
  14.0 102.8 %all-to-all-start = ((bf16[16,2,8192]{2,1,0:T(2,128)(2,1)}), bf16[16,2,8192]{2,1,0:T(2,128)(2,1)S(1)}, u32[]{:S(2)}, u32[]{:S(2)}) async-start(bf16[16,2,8192]{2,1,0:T(2,128)(2,1)} %reshape.260), calls=%async_computation | async-start | bytes 1048576 | tf_op jit(solution)/shard_map/all_to_all | solution.py:130
  20.5 7.8 copy-start.1
  30.1 5.8 copy-start.5
  116.8 126.4 %all-to-all-start.1 = ((bf16[3,256,4096]{1,0,2:T(4,128)(2,1)}), bf16[3,256,4096]{1,0,2:T(4,128)(2,1)}, u32[]{:S(2)}, u32[]{:S(2)}) async-start(bf16[3,256,4096]{1,0,2:T(4,128)(2,1)} %copy.123), calls=%async_computation.1 | async-start | bytes 16777216 | tf_op jit(solution)/shard_map/all_to_all | solution.py:111
  121.6 401.1 %all-reduce.2.cloned.1.call-start = ((), (), s32[]{:S(2)}) async-start(), calls=%async_computation.4 | async-start | bytes 8388608 | tf_op jit(solution)/shard_map/psum | solution.py:157
  141.3 9.0 %copy-start.7 = (bf16[7,4096]{1,0:T(8,128)(2,1)S(1)}, bf16[7,4096]{1,0:T(8,128)(2,1)}, u32[]{:S(2)}) copy-start(bf16[7,4096]{1,0:T(8,128)(2,1)} %param.33) | copy-start | bytes 172036
  160.7 10.7 %copy-start.4 = (bf16[5,512,4096]{1,2,0:T(8,128)(2,1)}, bf16[5,512,4096]{1,2,0:T(8,128)(2,1)S(1)}, u32[]{:S(2)}) copy-start(bf16[5,512,4096]{1,2,0:T(8,128)(2,1)S(1)} %add_convert_fusion) | copy-start | bytes 62914564
  160.7 10.7 %copy-start.16 = (s32[128]{0:T(128)S(1)}, s32[128]{0:T(128)}, u32[]{:S(2)}) copy-start(s32[128]{0:T(128)} %param.28) | copy-start | bytes 1540
  184.2 11.6 %copy-start.13 = (bf16[128,256]{1,0:T(8,128)(2,1)S(1)}, bf16[128,256]{1,0:T(8,128)(2,1)}, u32[]{:S(2)}) copy-start(bf16[128,256]{1,0:T(8,128)(2,1)} %param.36) | copy-start | bytes 196612
  184.2 11.6 %copy-start.14 = (f32[256]{0:T(256)S(1)}, f32[256]{0:T(256)}, u32[]{:S(2)}) copy-start(f32[256]{0:T(256)} %param.34) | copy-start | bytes 3076
  195.8 17.8 %copy-start.17 = (pred[512]{0:T(512)(128)(4,1)}, pred[512]{0:T(512)(128)(4,1)S(1)}, u32[]{:S(2)}) copy-start(pred[512]{0:T(512)(128)(4,1)S(1)} %iota_compare_fusion.1) | copy-start | bytes 1540
  265.7 20.9 %copy-start.12 = (pred[8,64]{1,0:T(8,128)(4,1)S(1)}, pred[8,64]{1,0:T(8,128)(4,1)}, u32[]{:S(2)}) copy-start(pred[8,64]{1,0:T(8,128)(4,1)} %add_compare_fusion) | copy-start | bytes 1540
  367.9 18.0 %copy-start.6 = (f32[4,64,64]{2,1,0:T(8,128)}, f32[4,64,64]{2,1,0:T(8,128)S(1)}, u32[]{:S(2)}) copy-start(f32[4,64,64]{2,1,0:T(8,128)S(1)} %get-tuple-element.47) | copy-start | bytes 196612
  367.9 8.4 %copy-start.15 = (f32[256]{0:T(256)S(1)}, f32[256]{0:T(256)}, u32[]{:S(2)}) copy-start(f32[256]{0:T(256)} %param.38) | copy-start | bytes 3076
  376.3 11.0 %copy-start.8 = (bf16[7,4096]{1,0:T(8,128)(2,1)S(1)}, bf16[7,4096]{1,0:T(8,128)(2,1)}, u32[]{:S(2)}) copy-start(bf16[7,4096]{1,0:T(8,128)(2,1)} %param.33) | copy-start | bytes 172036
  385.8 237.2 %all-gather.6.cloned.1.call-start = ((), (), s32[]{:S(2)}) async-start(), calls=%async_computation.5 | async-start | bytes 8257536 | tf_op jit(solution)/shard_map/all_gather | solution.py:167
  386.6 335.8 %all-gather.8.cloned.1.call-start = ((), (), s32[]{:S(2)}) async-start(), calls=%async_computation.6 | async-start | bytes 8257536 | tf_op jit(solution)/shard_map/all_gather | solution.py:168
  387.2 418.5 %reduce-scatter.2.cloned.1.call-start = ((), (), s32[]{:S(2)}) async-start(), calls=%async_computation.7 | async-start | bytes 4456448 | tf_op jit(solution)/shard_map/reduce_scatter | solution.py:174
  527.8 3.4 copy-start.3
  527.8 3.4 copy-start.10
  531.2 3.5 copy-start.2
  539.5 266.1 %copy-start.18 = (pred[512]{0:T(512)(128)(4,1)S(1)}, pred[512]{0:T(512)(128)(4,1)}, u32[]{:S(2)}) copy-start(pred[512]{0:T(512)(128)(4,1)} %copy-done.17) | copy-start | bytes 1540
Sparse Core Ops, SparseCore 0:
  10.8 92.8 all-gather.3
  386.0 136.6 all-reduce.1
  525.0 97.9 all-gather.5
  625.2 97.1 all-gather.7
  738.7 66.8 reduce-scatter.1
where the time goes:
time: 824 us; the launch traced here: 817 us
  waiting for transfers between devices  478 us (58%)
  local copies, waits for them, and re-layouts  128 us (16%)
  other arithmetic  122 us (15%)
  matrix products  59.3 us (7%)
  between operations  16.6 us (2%)
  starting transfers between devices  11.7 us (1%)
    psum x1, waiting for transfers between devices, local(): lax.psum(head_terms.astype(jnp.bfloat16), 'hid').astype(jnp.float32)  135 us
    all_gather x1, waiting for transfers between devices, local(): lax.all_gather(feedforward_exit_proj, 'req', axis=0, tiled=True)  99.4 us
    all_gather x1, waiting for transfers between devices, local(): key_rows = lax.all_gather(feedforward_entry_proj, 'req', axis=0, tiled=True)  83.5 us
    all_gather x1, waiting for transfers between devices, local(): collected = lax.all_gather(local_rows, 'req', axis=1, tiled=True)  67.1 us
    reduce_scatter x1, waiting for transfers between devices, local(): lax.psum_scatter(channel_terms.astype(jnp.bfloat16), 'hid', scatter_dimen...  64.5 us
    all_to_all x1, waiting for transfers between devices, local(): lax.all_to_all(collected, 'hid', split_axis=2, concat_axis=1, tiled=True)  27.1 us
    reduce_sum x8, other arithmetic, segment_step(): jnp.sum(acceptance_vectors[:, None] * factor * present_lookup_vectors[Non...  27 us
    gather x2, local copies, waits for them, and re-layouts, local(): jnp.take(blended[:3].reshape(3, seq_len, shards, shard_rows), partition_a...  23.5 us
  transfers between devices with their start and end apart: 7, of which 6 were waited for; matrix products, arithmetic and copies ran while one was open for 17% of the time, Pallas kernels for 0%

commit v1 on v0

--- a/solution.py
+++ b/solution.py
@@ -107,7 +107,9 @@
     local_rows = jnp.stack(
         [training_accept_pieces, training_lookup_pieces, training_content_pieces]
     ).astype(jnp.bfloat16)
-    collected = lax.all_gather(local_rows, "req", axis=1, tiled=True)
+    collected = jnp.concatenate(
+        lax.all_to_all(jnp.stack([local_rows] * lax.axis_size("req")), "req", 0, 0), axis=1
+    )
     swapped = lax.all_to_all(collected, "hid", split_axis=2, concat_axis=1, tiled=True)
     hid_count = lax.axis_size("hid")
     req_count = lax.axis_size("req")

time: 824 us -> 747 us (0.907)
  waiting for transfers between devices: 478 us -> 381 us
  local copies, waits for them, and re-layouts: 128 us -> 139 us
    all_gather x1, waiting for transfers between devices: 99.4 us -> 0.01 us  [local(): lax.all_gather(feedforward_exit_proj, 'req', axis=0, tiled=True)]
    all_gather x1, waiting for transfers between devices: 83.5 us -> 0.01 us  [local(): key_rows = lax.all_gather(feedforward_entry_proj, 'req', axis=0, tiled=True)]
    psum x1, waiting for transfers between devices: 135 us -> 218 us  [local(): lax.psum(head_terms.astype(jnp.bfloat16), 'hid').astype(jnp.float32)]
    all_gather x1 -> x0, waiting for transfers between devices: 67.1 us -> none  [local(): collected = lax.all_gather(local_rows, 'req', axis=1, tiled=True)]
    all_to_all x0 -> x1, waiting for transfers between devices: none -> 66.8 us  [local(): lax.all_to_all(jnp.stack([local_rows] * lax.axis_size('req')), 'req', 0, 0)]
    all_gather x1 -> x0, local copies, waits for them, and re-layouts: 13.1 us -> none  [local(): collected = lax.all_gather(local_rows, 'req', axis=1, tiled=True)]
    reshape x0 -> x1, local copies, waits for them, and re-layouts: none -> 13.1 us  [local(): jnp.concatenate(lax.all_to_all(jnp.stack([local_rows] * lax.axis_size('re...]
  transfers between devices with their start and end apart: 7 -> 7, of which waited for: 6 -> 4; matrix products, arithmetic and copies ran while one was open for 17% -> 19% of each run, Pallas kernels for 0% -> 0%
where the time goes in v1:
time: 747 us; the launch traced here: 738 us
  waiting for transfers between devices  381 us (51%)
  local copies, waits for them, and re-layouts  139 us (19%)
  other arithmetic  121 us (16%)
  matrix products  59.2 us (8%)
  starting transfers between devices  19.2 us (3%)
  between operations  18.1 us (2%)
    psum x1, waiting for transfers between devices, local(): lax.psum(head_terms.astype(jnp.bfloat16), 'hid').astype(jnp.float32)  218 us
    all_to_all x1, waiting for transfers between devices, local(): lax.all_to_all(jnp.stack([local_rows] * lax.axis_size('req')), 'req', 0, 0)  66.8 us
    reduce_scatter x1, waiting for transfers between devices, local(): lax.psum_scatter(channel_terms.astype(jnp.bfloat16), 'hid', scatter_dimen...  66.8 us
    all_to_all x1, waiting for transfers between devices, local(): lax.all_to_all(collected, 'hid', split_axis=2, concat_axis=1, tiled=True)  28.4 us
    reduce_sum x8, other arithmetic, segment_step(): jnp.sum(acceptance_vectors[:, None] * factor * present_lookup_vectors[Non...  27 us
    gather x2, local copies, waits for them, and re-layouts, local(): jnp.take(blended[:3].reshape(3, seq_len, shards, shard_rows), partition_a...  23.5 us
    dot_general x1, matrix products, local(): jnp.dot(hidden, value_rows, preferred_element_type=jnp.float32)  16.2 us
    all_to_all x2, local copies, waits for them, and re-layouts, local(): lax.all_to_all(collected, 'hid', split_axis=2, concat_axis=1, tiled=True)  15.9 us
  transfers between devices with their start and end apart: 7, of which 4 were waited for; matrix products, arithmetic and copies ran while one was open for 19% of the time, Pallas kernels for 0%

profile of v1, /device:TPU:6, one launch (start us, length us, event | category | flops | bytes accessed | tf_op | source)
XLA Modules:
  0.0 738.4 jit_solution(16997256432424297213)
XLA Ops:
  8.0 1.2 convert_bitcast_fusion.3
  9.2 1.3 convert_bitcast_fusion.1
  10.6 3.3 stack.36
  13.9 7.4 %all-to-all-start.1 = ((bf16[8,3,32,4096]{3,2,1,0:T(8,128)(2,1)}), bf16[8,3,32,4096]{3,2,1,0:T(8,128)(2,1)}, u32[]{:S(2)}, u32[]{:S(2)}) async-start(bf16[8,3,32,4096]{3,2,1,0:T(8,128)(2,1)} %stack.36), calls=%async_computation.1 | async-start | bytes 12582912 | tf_op jit(solution)/shard_map/all_to_all | solution.py:111
  22.1 1.8 fusion.60
  23.9 1.5 reshape.284
  25.4 3.0 convert_reduce_fusion
  28.3 3.4 fusion.19
  31.8 1.8 fusion.20
  33.7 3.3 copy-done.5
  37.0 3.8 slice_bitcast_fusion.1
  40.7 66.8 %all-to-all-done.1 = bf16[8,3,32,4096]{3,2,1,0:T(8,128)(2,1)} async-done(((bf16[8,3,32,4096]{3,2,1,0:T(8,128)(2,1)}), bf16[8,3,32,4096]{3,2,1,0:T(8,128)(2,1)}, u32[]{:S(2)}, u32[]{:S(2)}) %all-to-all-start.1) | async-done | bytes 6291488 | tf_op jit(solution)/shard_map/all_to_all | solution.py:111
  107.6 5.5 all-to-all-start
  113.7 6.1 copy.127
  119.9 13.1 %copy.128 = bf16[3,256,4096]{1,0,2:T(4,128)(2,1)} copy(bf16[3,256,4096]{2,1,0:T(8,128)(2,1)} %bitcast.196) | data formatting | bytes 12582912 | tf_op jit(solution)/shard_map/reshape | solution.py:110
  133.0 5.8 all-to-all-start.2
  139.1 10.4 %fusion.27 = (f32[512,4096]{1,0:T(8,128)}, f32[512,4096]{1,0:T(8,128)}) fusion(bf16[1,512,4096]{2,1,0:T(8,128)(2,1)} %param.24, f32[4096]{0:T(1024)S(1)} %bitcast.205, f32[512]{0:T(512)S(1)} %add_sqrt_fusion.1, f32[512]{0:T(512)S(1)} %broadcast_multiply_fusion.1, f32[1,511,4096]{2,1,0:T(8,128)} %slice_bitcast_fusion.1, f32[1,1,4096]{2,1,0:T(1,128)S(1)} %get-tuple-element.126), kind=kLoop, calls=%fused_computation.55 | loop fusion | flops 12582912 | bytes 29380608 | tf_op jit(solution)/shard_map/add | solution.py:101
  149.5 9.0 %copy.124 = f32[512,4096]{0,1:T(8,128)} copy(f32[512,4096]{1,0:T(8,128)} %get-tuple-element.120) | data formatting | bytes 16777216 | tf_op jit(solution)/shard_map/add | solution.py:101
  158.5 9.0 %copy.125 = f32[512,4096]{0,1:T(8,128)} copy(f32[512,4096]{1,0:T(8,128)} %get-tuple-element.121) | data formatting | bytes 16777216 | tf_op jit(solution)/shard_map/mul | solution.py:101
  167.5 10.3 %add_convert_fusion = bf16[5,512,4096]{1,2,0:T(8,128)(2,1)S(1)} fusion(f32[5,4096]{1,0:T(8,128)S(1)} %slice.75, f32[512,4096]{0,1:T(8,128)} %copy.125, f32[512,4096]{0,1:T(8,128)} %copy.124), kind=kLoop, calls=%fused_computation.28 | loop fusion | flops 31457280 | bytes 37830656 | tf_op jit(solution)/shard_map/convert_element_type | solution.py:101
  177.9 6.5 slice.77
  184.4 4.2 copy-done.4
  188.6 12.8 %gather_fusion = bf16[128,3,512,32]{2,3,1,0:T(8,128)(2,1)} fusion(bf16[3,512,128,32]{1,3,2,0:T(8,128)(2,1)} %bitcast.193, s32[1024]{0:T(1024)S(1)} %pad_clamp_fusion), kind=kCustom, calls=%fused_computation | custom fusion | bytes 25166336 | tf_op jit(solution)/shard_map/jit(_take)/gather | solution.py:104
  201.4 10.7 %copy.126 = bf16[3,512,128,32]{1,3,2,0:T(8,128)(2,1)} copy(bf16[3,512,128,32]{1,3,0,2:T(8,128)(2,1)} %bitcast.194) | data formatting | bytes 25165824 | tf_op jit(solution)/shard_map/jit(_take)/gather | solution.py:104
  213.0 3.9 fusion.34
  217.0 1.5 reshape.267
  219.6 11.2 %bitcast_select_fusion = bf16[3,512,4096]{1,2,0:T(8,128)(2,1)} fusion(bf16[3,512,128,32]{1,3,2,0:T(8,128)(2,1)} %copy.126, pred[4096]{0:T(1024)(128)(4,1)S(1)} %broadcast_in_dim.95), kind=kLoop, calls=%fused_computation.30 | loop fusion | flops 6291456 | bytes 25169920 | tf_op jit(solution)/shard_map/jit(_take)/select_n | solution.py:104
  230.8 1.7 reshape.285
  233.3 28.4 %all-to-all-done.2 = bf16[3,256,4096]{1,0,2:T(4,128)(2,1)} async-done(((bf16[3,256,4096]{1,0,2:T(4,128)(2,1)}), bf16[3,256,4096]{1,0,2:T(4,128)(2,1)}, u32[]{:S(2)}, u32[]{:S(2)}) %all-to-all-start.2) | async-done | bytes 6291488 | tf_op jit(solution)/shard_map/all_to_all | solution.py:113
  261.7 6.9 copy.129
  268.6 9.1 %copy.130 = bf16[3,16,256,256]{3,2,1,0:T(8,128)(2,1)} copy(bf16[3,16,256,256]{2,3,1,0:T(8,128)(2,1)} %bitcast.197) | data formatting | bytes 12582912 | tf_op jit(solution)/shard_map/all_to_all | solution.py:113
  277.7 6.5 copy.131
  284.1 12.0 %fusion.61 = f32[3,512,256]{2,1,0:T(8,128)} fusion(bf16[3,512,4096]{1,2,0:T(8,128)(2,1)} %bitcast_select_fusion, bf16[3,4096,256]{2,1,0:T(8,128)(2,1)} %bitcast.200), kind=kOutput, calls=%fused_computation.119 | convolution fusion | flops 3221225472 | bytes 20447232 | tf_op jit(solution)/shard_map/mtd,mdc->mtc/dot_general | solution.py:121
  296.1 2.5 fusion.58
  298.6 1.5 squeeze.51
  300.1 2.5 reshape_squeeze.6
  302.6 2.4 reshape_squeeze.7
  305.0 1.5 broadcast_select_fusion
  306.5 79.7 %while.12 = (s32[]{:T(128)}, f32[4,64,64]{2,1,0:T(8,128)S(1)}, f32[8,64,4,64]{3,1,2,0:T(8,128)}, f32[8,64,4,64]{3,2,1,0:T(4,128)}, f32[8,64,4,64]{3,2,1,0:T(4,12...) while((s32[]{:T(128)}, f32[4,64,64]{2,1,0:T(8,128)S(1)}, ...), condition=%wide.region_6.7_spmd, body=%wide.region_2.6_spmd.sunk | while | flops 45260544 | bytes 2537577 | solution.py:152
  307.2 1.1 multiply_reduce_fusion.5
  310.4 3.4 multiply_reduce_fusion.6
  320.4 3.4 multiply_reduce_fusion.6
  327.1 1.1 multiply_reduce_fusion.5
  330.3 3.4 multiply_reduce_fusion.6
  340.3 3.4 multiply_reduce_fusion.6
  347.0 1.1 multiply_reduce_fusion.5
  350.2 3.4 multiply_reduce_fusion.6
  360.1 3.4 multiply_reduce_fusion.6
  370.1 3.4 multiply_reduce_fusion.6
  380.1 3.4 multiply_reduce_fusion.6
  386.2 2.0 copy.135
  388.2 1.6 reduce_sum.74
  389.9 1.4 reshape.273
  391.3 1.9 multiply_reduce_fusion.2
  394.6 9.6 %convolution_convert_fusion.1 = bf16[512,4096]{1,0:T(8,128)(2,1)} fusion(bf16[256,4096]{1,0:T(8,128)(2,1)S(1)} %copy-done, bf16[4096,256]{1,0:T(8,128)(2,1)} %param.39, bf16[5,512,4096]{1,2,0:T(8,128)(2,1)} %copy-done.4, f32[512,256]{1,0:T(8,128)S(1)} %copy.140, f32[512,256]{1,0:T(8,128)} %reshape.273, f32[512,256]{1,0:T(8,128)} %copy.137, ...), kind=kOutput, calls=%fused_computation.54 | convolution fusion | flops 2150760448 | bytes 14156800 | tf_op jit(solution)/shard_map/dot_general | solution.py:158
  405.4 218.0 %all-reduce.2.cloned.1.call-done = bf16[512,4096]{1,0:T(8,128)(2,1)} async-done(((bf16[512,4096]{1,0:T(8,128)(2,1)}), bf16[512,4096]{1,0:T(8,128)(2,1)}) %all-reduce.2.cloned.1.call-update) | async-done | bytes 4194320 | tf_op jit(solution)/shard_map/psum | solution.py:159
  623.5 5.2 convert_reduce_fusion.1
  628.7 1.2 fusion.21
  629.9 2.1 fusion.22
  632.1 3.5 maximum_subtract_fusion.1
  635.5 4.8 add_convert_fusion.1
  640.4 16.2 %convolution_convert_fusion = bf16[512,4096]{1,0:T(8,128)(2,1)} fusion(bf16[896,4096]{1,0:T(8,128)(2,1)} %all-gather.5.cloned.1.call-done, bf16[896,4096]{1,0:T(8,128)(2,1)} %all-gather.3.cloned.1.call-done, bf16[2,512,4096]{2,1,0:T(8,128)(2,1)} %add_convert_fusion.1), kind=kOutput, calls=%fused_computation.53 | convolution fusion | flops 7519666176 | bytes 23068672 | tf_op jit(solution)/shard_map/dot_general | solution.py:175
  659.1 66.8 %reduce-scatter.2.cloned.1.call-done = bf16[512,256]{1,0:T(8,128)(2,1)} async-done(((bf16[512,4096]{1,0:T(8,128)(2,1)}), bf16[512,256]{1,0:T(8,128)(2,1)}) %reduce-scatter.2.cloned.1.call-update) | async-done | bytes 262160 | tf_op jit(solution)/shard_map/reduce_scatter | solution.py:176
  725.9 4.9 fusion.45
  (187 shorter events, 56.6 us)
Async XLA Ops:
  8.0 386.6 %copy-start = (bf16[256,4096]{1,0:T(8,128)(2,1)S(1)}, bf16[256,4096]{1,0:T(8,128)(2,1)}, u32[]{:S(2)}) copy-start(bf16[256,4096]{1,0:T(8,128)(2,1)} %param.40) | copy-start | bytes 6291460
  10.6 11.4 %copy-start.11 = (bf16[1,2,4096]{2,1,0:T(2,128)(2,1)S(1)}, bf16[1,2,4096]{2,1,0:T(2,128)(2,1)}, u32[]{:S(2)}) copy-start(bf16[1,2,4096]{2,1,0:T(2,128)(2,1)} %param.42) | copy-start | bytes 49156
  13.9 93.6 %all-to-all-start.1 = ((bf16[8,3,32,4096]{3,2,1,0:T(8,128)(2,1)}), bf16[8,3,32,4096]{3,2,1,0:T(8,128)(2,1)}, u32[]{:S(2)}, u32[]{:S(2)}) async-start(bf16[8,3,32,4096]{3,2,1,0:T(8,128)(2,1)} %stack.36), calls=%async_computation.1 | async-start | bytes 12582912 | tf_op jit(solution)/shard_map/all_to_all | solution.py:111
  21.4 10.4 %copy-start.9 = (bf16[2,4096]{1,0:T(2,128)(2,1)S(1)}, bf16[2,4096]{1,0:T(2,128)(2,1)}, u32[]{:S(2)}) copy-start(bf16[2,4096]{1,0:T(2,128)(2,1)} %param.32) | copy-start | bytes 49156
  25.4 6.4 copy-start.1
  33.7 3.3 copy-start.5
  107.6 25.4 %all-to-all-start = ((bf16[16,2,8192]{2,1,0:T(2,128)(2,1)}), bf16[16,2,8192]{2,1,0:T(2,128)(2,1)S(1)}, u32[]{:S(2)}, u32[]{:S(2)}) async-start(bf16[16,2,8192]{2,1,0:T(2,128)(2,1)} %reshape.284), calls=%async_computation | async-start | bytes 1048576 | tf_op jit(solution)/shard_map/all_to_all | solution.py:132
  133.0 128.7 %all-to-all-start.2 = ((bf16[3,256,4096]{1,0,2:T(4,128)(2,1)}), bf16[3,256,4096]{1,0,2:T(4,128)(2,1)}, u32[]{:S(2)}, u32[]{:S(2)}) async-start(bf16[3,256,4096]{1,0,2:T(4,128)(2,1)} %copy.128), calls=%async_computation.2 | async-start | bytes 16777216 | tf_op jit(solution)/shard_map/all_to_all | solution.py:113
  138.8 484.7 %all-reduce.2.cloned.1.call-start = ((), (), s32[]{:S(2)}) async-start(), calls=%async_computation.4 | async-start | bytes 8388608 | tf_op jit(solution)/shard_map/psum | solution.py:159
  158.5 9.0 %copy-start.7 = (bf16[7,4096]{1,0:T(8,128)(2,1)S(1)}, bf16[7,4096]{1,0:T(8,128)(2,1)}, u32[]{:S(2)}) copy-start(bf16[7,4096]{1,0:T(8,128)(2,1)} %param.33) | copy-start | bytes 172036
  177.8 10.7 %copy-start.4 = (bf16[5,512,4096]{1,2,0:T(8,128)(2,1)}, bf16[5,512,4096]{1,2,0:T(8,128)(2,1)S(1)}, u32[]{:S(2)}) copy-start(bf16[5,512,4096]{1,2,0:T(8,128)(2,1)S(1)} %add_convert_fusion) | copy-start | bytes 62914564
  177.9 10.7 %copy-start.16 = (s32[128]{0:T(128)S(1)}, s32[128]{0:T(128)}, u32[]{:S(2)}) copy-start(s32[128]{0:T(128)} %param.28) | copy-start | bytes 1540
  201.4 11.6 %copy-start.13 = (bf16[128,256]{1,0:T(8,128)(2,1)S(1)}, bf16[128,256]{1,0:T(8,128)(2,1)}, u32[]{:S(2)}) copy-start(bf16[128,256]{1,0:T(8,128)(2,1)} %param.36) | copy-start | bytes 196612
  201.4 11.6 %copy-start.14 = (f32[256]{0:T(256)S(1)}, f32[256]{0:T(256)}, u32[]{:S(2)}) copy-start(f32[256]{0:T(256)} %param.34) | copy-start | bytes 3076
  213.0 17.8 %copy-start.17 = (pred[512]{0:T(512)(128)(4,1)}, pred[512]{0:T(512)(128)(4,1)S(1)}, u32[]{:S(2)}) copy-start(pred[512]{0:T(512)(128)(4,1)S(1)} %iota_compare_fusion.1) | copy-start | bytes 1540
  284.1 20.9 %copy-start.12 = (pred[8,64]{1,0:T(8,128)(4,1)S(1)}, pred[8,64]{1,0:T(8,128)(4,1)}, u32[]{:S(2)}) copy-start(pred[8,64]{1,0:T(8,128)(4,1)} %add_compare_fusion) | copy-start | bytes 1540
  386.2 17.9 %copy-start.6 = (f32[4,64,64]{2,1,0:T(8,128)}, f32[4,64,64]{2,1,0:T(8,128)S(1)}, u32[]{:S(2)}) copy-start(f32[4,64,64]{2,1,0:T(8,128)S(1)} %get-tuple-element.47) | copy-start | bytes 196612
  386.2 8.4 %copy-start.15 = (f32[256]{0:T(256)S(1)}, f32[256]{0:T(256)}, u32[]{:S(2)}) copy-start(f32[256]{0:T(256)} %param.38) | copy-start | bytes 3076
  394.6 10.8 %copy-start.8 = (bf16[7,4096]{1,0:T(8,128)(2,1)S(1)}, bf16[7,4096]{1,0:T(8,128)(2,1)}, u32[]{:S(2)}) copy-start(bf16[7,4096]{1,0:T(8,128)(2,1)} %param.33) | copy-start | bytes 172036
  404.2 236.2 %all-gather.3.cloned.1.call-start = ((), (), s32[]{:S(2)}) async-start(), calls=%async_computation.5 | async-start | bytes 8257536 | tf_op jit(solution)/shard_map/all_gather | solution.py:169
  404.8 235.6 %all-gather.5.cloned.1.call-start = ((), (), s32[]{:S(2)}) async-start(), calls=%async_computation.6 | async-start | bytes 8257536 | tf_op jit(solution)/shard_map/all_gather | solution.py:170
  405.4 320.6 %reduce-scatter.2.cloned.1.call-start = ((), (), s32[]{:S(2)}) async-start(), calls=%async_computation.7 | async-start | bytes 4456448 | tf_op jit(solution)/shard_map/reduce_scatter | solution.py:176
  628.6 3.4 copy-start.3
  628.7 3.4 copy-start.10
  632.0 3.5 copy-start.2
  640.4 85.6 %copy-start.18 = (pred[512]{0:T(512)(128)(4,1)S(1)}, pred[512]{0:T(512)(128)(4,1)}, u32[]{:S(2)}) copy-start(pred[512]{0:T(512)(128)(4,1)} %copy-done.17) | copy-start | bytes 1540
Sparse Core Ops, SparseCore 0:
  404.3 219.1 all-reduce.1
  656.7 69.1 reduce-scatter.1
Sparse Core Ops, SparseCore 1:
  407.0 103.4 all-gather.2
  512.6 96.7 all-gather.4
